TPU v7x, 256 devices: a whole 4x4x8 slice. The times are simulated.
256 devices in a mesh: ctx: 32 (over x, y, core), head: 8 (over z).
Axes of the slice: x: 4, y: 4, z: 8, core: 2. Of those that a mesh axis runs over, the one named last changes fastest.
Arguments:
- queries: bfloat16 [8192, 8192], P('ctx', 'head'), may hold values from -110 to 110
- keys: bfloat16 [8192, 1024], P('ctx', 'head'), may hold values from -3.1 to 3.1
- values: bfloat16 [8192, 1024], P('ctx', 'head'), may hold values from -6 to 6
- cf_queries: bfloat16 [8192, 8192], P('ctx', 'head'), may hold values from -6 to 6
- cf_keys: bfloat16 [8192, 1024], P('ctx', 'head'), may hold values from -6 to 6
- cf_values: bfloat16 [8192, 1024], P('ctx', 'head'), may hold values from -6 to 6
- patch_source: int32 [8192], replicated, may hold values from -1 to 8191, as said below
- doc_lengths: int32 [32], replicated, may hold values from 1 to 4608, as said below
- out_weight: bfloat16 [8192, 4096], P('head'), may hold values from -0.5 to 0.5
Outputs:
- attn_out: bfloat16 [8192, 4096], P(('ctx', 'head'))
Inputs may be any that keep to these rules, and one draw needn't show every extreme that they name: `patch_source`: exactly one aligned block of 128 positions of each index of ctx is replaced; its rows come from 16 different indices of ctx, 8 consecutive rows from each; no counterfactual position is used twice. `doc_lengths`: the lengths sum to 8192, and one document has exactly 4608 positions.
All inputs are finite; a program needn't handle non-finite values.
Results may differ from a plain program's by a relative error of at most 0.014.
Values may be sent and summed in bfloat16 or wider, within the bound.
A program may use at most 192 MiB of HBM per device.

v0:
```python
import math
import jax
import jax.numpy as jnp
from jax import lax
from jax.sharding import PartitionSpec as P

HD = 128
BLK = 128


def attend_block(running, pieces, grouped, query_pos, query_doc, doc_ends):
    row_max, row_sum, weighted = running
    key_piece, value_piece = pieces
    piece_rows = key_piece.shape[0]
    kv_heads = grouped.shape[1]
    key_heads = key_piece.reshape(piece_rows, kv_heads, HD)
    value_heads = value_piece.reshape(piece_rows, kv_heads, HD)
    scores = jnp.einsum(
        "qhgd,khd->hgqk", grouped, key_heads, preferred_element_type=jnp.float32
    ) * (1.0 / math.sqrt(HD))
    key_pos = jnp.arange(piece_rows, dtype=jnp.int32)
    key_doc = jnp.sum((key_pos[:, None] >= doc_ends[None, :]).astype(jnp.int32), axis=1)
    visible = (
        (query_pos[:, None] >= key_pos[None, :])
        & (query_doc[:, None] == key_doc[None, :])
        & (key_pos[None, :] >= 0)
    )
    scores = jnp.where(visible, scores, -jnp.inf)
    new_max = jnp.max(scores, axis=-1)
    safe_max = jnp.where(new_max == -jnp.inf, 0.0, new_max)
    rescale = jnp.exp(row_max - safe_max)
    weights = jnp.exp(scores - safe_max[..., None])
    row_sum = row_sum * rescale + jnp.sum(weights, axis=-1)
    weighted = weighted * rescale[..., None] + jnp.einsum(
        "hgqk,khd->hgqd",
        weights.astype(jnp.bfloat16),
        value_heads,
        preferred_element_type=jnp.float32,
    )
    return (new_max, row_sum, weighted)


def per_device(
    queries, keys, values, cf_queries, cf_keys, cf_values, patch_source, doc_lengths, out_weight
):
    ctx_size = lax.axis_size("ctx")
    my_index = lax.axis_index("ctx")
    local_rows = queries.shape[0]
    group_count = min(ctx_size, 16)
    slot_cap = BLK // group_count
    source_grid = patch_source.reshape(ctx_size, local_rows)
    owner_dev = jnp.where(source_grid >= 0, source_grid // local_rows, -1)
    from_me = (owner_dev == my_index).astype(jnp.int32)
    slot_rank = jnp.cumsum(from_me, axis=1) - 1
    slot_index = jnp.arange(ctx_size, dtype=jnp.int32)[:, None] * slot_cap + slot_rank
    slot_index = jnp.where(from_me > 0, slot_index, ctx_size * slot_cap)
    local_source = jnp.clip(source_grid - my_index * local_rows, 0, local_rows - 1)
    send_table = (
        jnp.zeros((ctx_size * slot_cap,), jnp.int32)
        .at[slot_index.reshape(-1)]
        .set(local_source.reshape(-1), mode="drop")
    )
    send_queries = cf_queries[send_table].reshape(ctx_size, slot_cap, cf_queries.shape[1])
    send_keys = cf_keys[send_table].reshape(ctx_size, slot_cap, cf_keys.shape[1])
    send_values = cf_values[send_table].reshape(ctx_size, slot_cap, cf_values.shape[1])
    recv_queries, recv_keys, recv_values = (
        lax.all_to_all(send_queries, "ctx", split_axis=0, concat_axis=0, tiled=True),
        lax.all_to_all(send_keys, "ctx", split_axis=0, concat_axis=0, tiled=True),
        lax.all_to_all(send_values, "ctx", split_axis=0, concat_axis=0, tiled=True),
    )
    own_source = lax.dynamic_slice_in_dim(patch_source, my_index * local_rows, local_rows)
    patched = own_source >= 0
    source_dev = jnp.where(patched, own_source // local_rows, -1)
    source_hit = (source_dev[:, None] == jnp.arange(ctx_size, dtype=jnp.int32)[None, :]).astype(
        jnp.int32
    )
    earlier = jnp.cumsum(source_hit, axis=0) - source_hit
    recv_rank = jnp.sum(earlier * source_hit, axis=1)
    pick_slot = jnp.clip(source_dev * slot_cap + recv_rank, 0, ctx_size * slot_cap - 1)
    query_rows = jnp.where(
        patched[:, None], recv_queries.reshape(ctx_size * slot_cap, -1)[pick_slot], queries
    )
    key_rows = jnp.where(
        patched[:, None], recv_keys.reshape(ctx_size * slot_cap, -1)[pick_slot], keys
    )
    value_rows = jnp.where(
        patched[:, None], recv_values.reshape(ctx_size * slot_cap, -1)[pick_slot], values
    )
    kv_heads = keys.shape[1] // HD
    query_heads = queries.shape[1] // HD
    group_size = query_heads // kv_heads
    grouped = query_rows.reshape(local_rows, kv_heads, group_size, HD)
    doc_ends = jnp.cumsum(doc_lengths)
    query_pos = my_index * local_rows + jnp.arange(local_rows, dtype=jnp.int32)
    query_doc = jnp.sum((query_pos[:, None] >= doc_ends[None, :]).astype(jnp.int32), axis=1)
    initial = (
        jnp.full((kv_heads, group_size, local_rows), -jnp.inf, jnp.float32),
        jnp.zeros((kv_heads, group_size, local_rows), jnp.float32),
        jnp.zeros((kv_heads, group_size, local_rows, HD), jnp.float32),
    )
    pieces = (
        lax.all_gather(key_rows, "ctx", axis=0, tiled=True),
        lax.all_gather(value_rows, "ctx", axis=0, tiled=True),
    )
    first_row = jnp.int32(0)
    piece_rows = pieces[0].shape[0]
    last_doc = jnp.sum((first_row + piece_rows - 1 >= doc_ends).astype(jnp.int32))
    reaches = (first_row <= query_pos[local_rows - 1]) & (last_doc >= query_doc[0])

    def compute_block(previous):
        return attend_block(previous, pieces, grouped, query_pos, query_doc, doc_ends)

    def keep_block(previous):
        return previous

    running = lax.cond(reaches, compute_block, keep_block, initial)
    row_max, row_sum, weighted = running
    normalized = weighted / row_sum[..., None]
    attended = (
        jnp.transpose(normalized, (2, 0, 1, 3))
        .reshape(local_rows, query_heads * HD)
        .astype(jnp.bfloat16)
    )
    return lax.psum_scatter(
        jnp.dot(attended, out_weight, preferred_element_type=jnp.float32).astype(jnp.bfloat16),
        "head",
        scatter_dimension=0,
        tiled=True,
    )


def solution(mesh):
    in_specs = (
        P("ctx", "head"),
        P("ctx", "head"),
        P("ctx", "head"),
        P("ctx", "head"),
        P("ctx", "head"),
        P("ctx", "head"),
        P(),
        P(),
        P("head", None),
    )
    out_specs = P(("ctx", "head"), None)
    return jax.shard_map(
        per_device, mesh=mesh, in_specs=in_specs, out_specs=out_specs, check_vma=False
    )
```

profile of v0, /device:TPU:2, one launch (start us, length us, event | category | flops | bytes accessed | tf_op | source)
XLA Modules:
  0.0 307.0 jit_solution(17223273761956999939)
XLA Ops:
  9.2 30.4 %scatter_custom_fusion = s32[256]{0:T(256)S(1)} fusion(s32[8192]{0:T(1024)S(1)} %get-tuple-element.51, s32[8192]{0:T(1024)S(1)} %get-tuple-element.50, s32[]{:T(128)} %constant.69.clone.1), kind=kCustom, calls=%fused_computation.90 | custom fusion | bytes 1028 | tf_op jit(solution)/shard_map/scatter | solution.py:61
  39.7 2.2 gather_fusion.4
  41.9 7.6 %all-to-all-start.2 = ((bf16[32,8,128]{2,1,0:T(8,128)(2,1)}), bf16[32,8,128]{2,1,0:T(8,128)(2,1)S(1)}, u32[]{:S(2)}, u32[]{:S(2)}) async-start(bf16[32,8,128]{2,1,0:T(8,128)(2,1)} %bitcast.22), calls=%async_computation.2 | async-start | bytes 131072 | tf_op jit(solution)/shard_map/all_to_all | solution.py:69
  51.2 2.2 gather_fusion.2
  53.4 2.4 all-to-all-done.2
  55.8 5.0 %all-to-all-start.1 = ((bf16[32,8,128]{2,1,0:T(8,128)(2,1)}), bf16[32,8,128]{2,1,0:T(8,128)(2,1)S(1)}, u32[]{:S(2)}, u32[]{:S(2)}) async-start(bf16[32,8,128]{2,1,0:T(8,128)(2,1)} %bitcast.20), calls=%async_computation.1 | async-start | bytes 131072 | tf_op jit(solution)/shard_map/all_to_all | solution.py:68
  60.9 0.9 gather_fusion.5
  61.7 5.5 %all-to-all-done.1 = bf16[32,8,128]{2,1,0:T(8,128)(2,1)S(1)} async-done(((bf16[32,8,128]{2,1,0:T(8,128)(2,1)}), bf16[32,8,128]{2,1,0:T(8,128)(2,1)S(1)}, u32[]{:S(2)}, u32[]{:S(2)}) %all-to-all-start.1) | async-done | bytes 65568 | tf_op jit(solution)/shard_map/all_to_all | solution.py:68
  68.1 1.6 broadcast_select_fusion
  70.5 2.0 gather_fusion.1
  72.4 5.0 %all-to-all-start = ((bf16[32,8,1024]{2,1,0:T(8,128)(2,1)}), bf16[32,8,1024]{2,1,0:T(8,128)(2,1)S(1)}, u32[]{:S(2)}, u32[]{:S(2)}) async-start(bf16[32,8,1024]{2,1,0:T(8,128)(2,1)} %bitcast.16), calls=%async_computation | async-start | bytes 1048576 | tf_op jit(solution)/shard_map/all_to_all | solution.py:67
  82.5 4.8 %all-to-all-done = bf16[32,8,1024]{2,1,0:T(8,128)(2,1)S(1)} async-done(((bf16[32,8,1024]{2,1,0:T(8,128)(2,1)}), bf16[32,8,1024]{2,1,0:T(8,128)(2,1)S(1)}, u32[]{:S(2)}, u32[]{:S(2)}) %all-to-all-start) | async-done | bytes 524320 | tf_op jit(solution)/shard_map/all_to_all | solution.py:67
  87.3 31.8 %all-gather.5.cloned.1.call-done = bf16[8192,128]{1,0:T(8,128)(2,1)} async-done(((bf16[256,128]{1,0:T(8,128)(2,1)}), bf16[8192,128]{1,0:T(8,128)(2,1)}) %all-gather.5.cloned.1.call-update) | async-done | bytes 2097168 | tf_op jit(solution)/shard_map/all_gather | solution.py:103
  119.1 50.6 %all-gather.3.cloned.1.call-done = bf16[8192,128]{1,0:T(8,128)(2,1)} async-done(((bf16[256,128]{1,0:T(8,128)(2,1)}), bf16[8192,128]{1,0:T(8,128)(2,1)}) %all-gather.3.cloned.1.call-update) | async-done | bytes 2097168 | tf_op jit(solution)/shard_map/all_gather | solution.py:102
  169.7 79.6 %conditional.1 = (f32[1,8,256]{2,1,0:T(8,128)S(1)}, f32[1,8,256,128]{2,3,1,0:T(8,128)}) conditional(s32[]{:T(128)} %convert_element_type.43, () %tuple.13, (s32[256]{0:T(256)S(1)}, s32[256]{0:T(256)S(1)}, s32[32]{0:T(128)S(1)}, pred[256]{0:T(512)(128)(4,1)S(1)}, bf16[32,8,1024]{2,1,0:T(8,128)(2,1)S(1)}, /*index=5*/s32[256,1]{0,1:T(1,128)S(1)}, ...), branch_computations={%region_9.10_spmd, %region_10.14_spmd} | conditional | flops 8782093312 | bytes 219316624 | solution.py:116
  169.7 1.2 gather_fusion
  171.1 1.9 fusion.7
  173.0 25.8 %fusion.2 = (f32[8,256]{1,0:T(8,128)S(1)}, f32[256,8,8192]{2,0,1:T(8,128)}) fusion(pred[256,8192]{1,0:T(8,128)(4,1)S(1)} %fusion.7, bf16[8192,128]{1,0:T(8,128)(2,1)} %get-tuple-element.35, bf16[256,1024]{1,0:T(8,128)(2,1)S(1)} %gather_fusion, bf16[256,1024]{1,0:T(8,128)(2,1)} %get-tuple-element.42, pred[256]{0:T(512)(128)(4,1)S(1)} %get-tuple-element.31), kind=kOutput, calls=%fused_computation.11 | convolution fusion | flops 4345559040 | bytes 72360192 | tf_op jit(solution)/shard_map/cond/branch_1_fun/qhgd,khd->hgqk/dot_general | solution.py:18
  198.8 26.2 %fusion.16 = f32[1,8,256,128]{3,2,1,0:T(8,128)} fusion(bf16[8192,128]{1,0:T(8,128)(2,1)} %get-tuple-element.36, f32[256,8,8192]{2,0,1:T(8,128)} %get-tuple-element.49, f32[8,256]{1,0:T(8,128)S(1)} %get-tuple-element.47, pred[256,8192]{1,0:T(8,128)(4,1)S(1)} %fusion.7, f32[8,256]{1,0:T(8,128)S(1)} %get-tuple-element.46), kind=kOutput, calls=%fused_computation.21 | convolution fusion | flops 4362338304 | bytes 72368128 | tf_op jit(solution)/shard_map/cond/branch_1_fun/hgqk,khd->hgqd/dot_general | solution.py:34
  225.0 21.8 %fusion.1 = f32[8,256]{1,0:T(8,128)S(1)} fusion(f32[256,8,8192]{2,0,1:T(8,128)} %get-tuple-element.49, f32[8,256]{1,0:T(8,128)S(1)} %get-tuple-element.47, pred[256,8192]{1,0:T(8,128)(4,1)S(1)} %fusion.7), kind=kLoop, calls=%fused_computation.10 | loop fusion | flops 67106816 | bytes 69222400 | tf_op jit(solution)/shard_map/cond/branch_1_fun/reduce_sum | solution.py:33
  246.8 2.6 copy.34
  249.3 1.3 divide_convert_fusion
  250.7 7.1 %convolution_convert_fusion = bf16[256,4096]{1,0:T(8,128)(2,1)} fusion(bf16[256,1024]{0,1:T(8,128)(2,1)S(1)} %bitcast.99, bf16[1024,4096]{1,0:T(8,128)(2,1)} %param.19), kind=kOutput, calls=%fused_computation.37 | convolution fusion | flops 2148532224 | bytes 11010048 | tf_op jit(solution)/shard_map/dot_general | solution.py:125
  257.8 42.7 %reduce-scatter.2.cloned.1.call-done = bf16[32,4096]{1,0:T(8,128)(2,1)} async-done(((bf16[256,4096]{1,0:T(8,128)(2,1)}), bf16[32,4096]{1,0:T(8,128)(2,1)}) %reduce-scatter.2.cloned.1.call-update) | async-done | bytes 262160 | tf_op jit(solution)/shard_map/reduce_scatter | solution.py:124
  (43 shorter events, 9.3 us)
Async XLA Ops:
  6.5 63.9 %copy-start = (bf16[256,1024]{1,0:T(8,128)(2,1)S(1)}, bf16[256,1024]{1,0:T(8,128)(2,1)}, u32[]{:S(2)}) copy-start(bf16[256,1024]{1,0:T(8,128)(2,1)} %param.14) | copy-start | bytes 1572868
  41.9 14.0 %all-to-all-start.2 = ((bf16[32,8,128]{2,1,0:T(8,128)(2,1)}), bf16[32,8,128]{2,1,0:T(8,128)(2,1)S(1)}, u32[]{:S(2)}, u32[]{:S(2)}) async-start(bf16[32,8,128]{2,1,0:T(8,128)(2,1)} %bitcast.22), calls=%async_computation.2 | async-start | bytes 131072 | tf_op jit(solution)/shard_map/all_to_all | solution.py:69
  55.8 11.4 %all-to-all-start.1 = ((bf16[32,8,128]{2,1,0:T(8,128)(2,1)}), bf16[32,8,128]{2,1,0:T(8,128)(2,1)S(1)}, u32[]{:S(2)}, u32[]{:S(2)}) async-start(bf16[32,8,128]{2,1,0:T(8,128)(2,1)} %bitcast.20), calls=%async_computation.1 | async-start | bytes 131072 | tf_op jit(solution)/shard_map/all_to_all | solution.py:68
  60.8 58.3 %all-gather.5.cloned.1.call-start = ((), (), s32[]{:S(2)}) async-start(), calls=%async_computation.5 | async-start | bytes 2162688 | tf_op jit(solution)/shard_map/all_gather | solution.py:103
  69.7 100.0 %all-gather.3.cloned.1.call-start = ((), (), s32[]{:S(2)}) async-start(), calls=%async_computation.4 | async-start | bytes 2162688 | tf_op jit(solution)/shard_map/all_gather | solution.py:102
  72.4 14.9 %all-to-all-start = ((bf16[32,8,1024]{2,1,0:T(8,128)(2,1)}), bf16[32,8,1024]{2,1,0:T(8,128)(2,1)S(1)}, u32[]{:S(2)}, u32[]{:S(2)}) async-start(bf16[32,8,1024]{2,1,0:T(8,128)(2,1)} %bitcast.16), calls=%async_computation | async-start | bytes 1048576 | tf_op jit(solution)/shard_map/all_to_all | solution.py:67
  77.5 223.0 %reduce-scatter.2.cloned.1.call-start = ((), (), s32[]{:S(2)}) async-start(), calls=%async_computation.6 | async-start | bytes 2359296 | tf_op jit(solution)/shard_map/reduce_scatter | solution.py:124
Sparse Core Ops, SparseCore 0:
  69.8 49.2 all-gather.4
  121.7 47.9 all-gather.2
  257.9 42.5 reduce-scatter.1
where the time goes:
time: 308 us; the launch traced here: 307 us
  waiting for transfers between devices  139 us (45%)
  matrix products  59.1 us (19%)
  local copies, waits for them, and re-layouts  44.7 us (15%)
  other arithmetic  31.7 us (10%)
  starting transfers between devices  17.7 us (6%)
  between operations  15.3 us (5%)
    all_gather x1, waiting for transfers between devices, per_device(): lax.all_gather(key_rows, 'ctx', axis=0, tiled=True)  50.6 us
    reduce_scatter x1, waiting for transfers between devices, per_device(): lax.psum_scatter(jnp.dot(attended, out_weight, preferred_element_type=jnp...  42.7 us
    all_gather x1, waiting for transfers between devices, per_device(): lax.all_gather(value_rows, 'ctx', axis=0, tiled=True)  31.8 us
    scatter x1, local copies, waits for them, and re-layouts, per_device(): send_table = jnp.zeros((ctx_size * slot_cap,), jnp.int32).at[slot_index.r...  30.4 us
    dot_general x1, matrix products, attend_block(): jnp.einsum('hgqk,khd->hgqd', weights.astype(jnp.bfloat16), value_heads, p...  26.2 us
    dot_general x1, matrix products, attend_block(): jnp.einsum('qhgd,khd->hgqk', grouped, key_heads, preferred_element_type=j...  25.8 us
    reduce_sum x1, other arithmetic, attend_block(): row_sum = row_sum * rescale + jnp.sum(weights, axis=-1)  21.8 us
    all_to_all x1, starting transfers between devices, per_device(): lax.all_to_all(send_values, 'ctx', split_axis=0, concat_axis=0, tiled=True)  7.62 us
  transfers between devices with their start and end apart: 6, of which 6 were waited for; matrix products, arithmetic and copies ran while one was open for 3% of the time, Pallas kernels for 0%

commit v1 on v0

--- a/solution.py
+++ b/solution.py
@@ -98,10 +98,13 @@
         jnp.zeros((kv_heads, group_size, local_rows), jnp.float32),
         jnp.zeros((kv_heads, group_size, local_rows, HD), jnp.float32),
     )
-    pieces = (
-        lax.all_gather(key_rows, "ctx", axis=0, tiled=True),
-        lax.all_gather(value_rows, "ctx", axis=0, tiled=True),
+    report_chunk = lambda local_array, dim_no: jnp.concatenate(
+        lax.all_to_all(
+            jnp.stack([local_array for _ in range(lax.axis_size("ctx"))], 0), "ctx", 0, 0
+        ),
+        dim_no,
     )
+    pieces = (report_chunk(key_rows, 0), lax.all_gather(value_rows, "ctx", axis=0, tiled=True))
     first_row = jnp.int32(0)
     piece_rows = pieces[0].shape[0]
     last_doc = jnp.sum((first_row + piece_rows - 1 >= doc_ends).astype(jnp.int32))

time: 308 us -> 268 us (0.87)
  waiting for transfers between devices: 139 us -> 81.2 us
  blocking collectives: 0 us -> 14.3 us
    all_gather x1 -> x0, waiting for transfers between devices: 50.6 us -> none  [per_device(): lax.all_gather(key_rows, 'ctx', axis=0, tiled=True)]
    all_gather x1, waiting for transfers between devices: 31.8 us -> 5.46 us  [per_device(): lax.all_gather(value_rows, 'ctx', axis=0, tiled=True)]
    all_to_all x1, waiting for transfers between devices: 4.82 us -> 23.8 us  [per_device(): lax.all_to_all(jnp.stack([local_array for _ in range(lax.axis_size('ctx')...]
    all_to_all x0 -> x1, blocking collectives: none -> 14.3 us  [per_device(): lax.all_to_all(send_queries, 'ctx', split_axis=0, concat_axis=0, tiled=True)]
  transfers between devices with their start and end apart: 6 -> 5, of which waited for: 6 -> 5; matrix products, arithmetic and copies ran while one was open for 3% -> 4% of each run, Pallas kernels for 0% -> 0%
where the time goes in v1:
time: 268 us; the launch traced here: 267 us
  waiting for transfers between devices  81.2 us (30%)
  matrix products  60.3 us (22%)
  local copies, waits for them, and re-layouts  46.4 us (17%)
  other arithmetic  31.6 us (12%)
  starting transfers between devices  18.1 us (7%)
  between operations  15.4 us (6%)
  blocking collectives  14.3 us (5%)
    reduce_scatter x1, waiting for transfers between devices, per_device(): lax.psum_scatter(jnp.dot(attended, out_weight, preferred_element_type=jnp...  44.1 us
    scatter x1, local copies, waits for them, and re-layouts, per_device(): send_table = jnp.zeros((ctx_size * slot_cap,), jnp.int32).at[slot_index.r...  30.4 us
    dot_general x1, matrix products, attend_block(): jnp.einsum('qhgd,khd->hgqk', grouped, key_heads, preferred_element_type=j...  26.9 us
    dot_general x1, matrix products, attend_block(): jnp.einsum('hgqk,khd->hgqd', weights.astype(jnp.bfloat16), value_heads, p...  26.3 us
    all_to_all x1, waiting for transfers between devices, per_device(): lax.all_to_all(jnp.stack([local_array for _ in range(lax.axis_size('ctx')...  23.8 us
    reduce_sum x1, other arithmetic, attend_block(): row_sum = row_sum * rescale + jnp.sum(weights, axis=-1)  21.8 us
    all_to_all x1, blocking collectives, per_device(): lax.all_to_all(send_queries, 'ctx', split_axis=0, concat_axis=0, tiled=True)  14.3 us
    all_to_all x1, starting transfers between devices, per_device(): lax.all_to_all(send_values, 'ctx', split_axis=0, concat_axis=0, tiled=True)  7.62 us
  transfers between devices with their start and end apart: 5, of which 5 were waited for; matrix products, arithmetic and copies ran while one was open for 4% of the time, Pallas kernels for 0%

profile of v1, /device:TPU:2, one launch (start us, length us, event | category | flops | bytes accessed | tf_op | source)
XLA Modules:
  0.0 267.4 jit_solution(4946922148047427218)
XLA Ops:
  9.2 30.4 %scatter_custom_fusion = s32[256]{0:T(256)S(1)} fusion(s32[8192]{0:T(1024)S(1)} %get-tuple-element.51, s32[8192]{0:T(1024)S(1)} %get-tuple-element.50, s32[]{:T(128)} %constant.69.clone.1), kind=kCustom, calls=%fused_computation.89 | custom fusion | bytes 1028 | tf_op jit(solution)/shard_map/scatter | solution.py:61
  39.7 2.2 gather_fusion.4
  41.9 7.6 %all-to-all-start.3 = ((bf16[32,8,128]{2,1,0:T(8,128)(2,1)}), bf16[32,8,128]{2,1,0:T(8,128)(2,1)S(1)}, u32[]{:S(2)}, u32[]{:S(2)}) async-start(bf16[32,8,128]{2,1,0:T(8,128)(2,1)} %bitcast.23), calls=%async_computation.3 | async-start | bytes 131072 | tf_op jit(solution)/shard_map/all_to_all | solution.py:69
  51.2 2.2 gather_fusion.2
  53.4 2.4 all-to-all-done.3
  55.8 5.0 %all-to-all-start.1 = ((bf16[32,8,128]{2,1,0:T(8,128)(2,1)}), bf16[32,8,128]{2,1,0:T(8,128)(2,1)S(1)}, u32[]{:S(2)}, u32[]{:S(2)}) async-start(bf16[32,8,128]{2,1,0:T(8,128)(2,1)} %bitcast.21), calls=%async_computation.1 | async-start | bytes 131072 | tf_op jit(solution)/shard_map/all_to_all | solution.py:68
  61.7 5.5 %all-to-all-done.1 = bf16[32,8,128]{2,1,0:T(8,128)(2,1)S(1)} async-done(((bf16[32,8,128]{2,1,0:T(8,128)(2,1)}), bf16[32,8,128]{2,1,0:T(8,128)(2,1)S(1)}, u32[]{:S(2)}, u32[]{:S(2)}) %all-to-all-start.1) | async-done | bytes 65568 | tf_op jit(solution)/shard_map/all_to_all | solution.py:68
  68.1 1.6 broadcast_select_fusion
  69.7 1.2 gather_fusion.1
  70.9 14.3 %all_to_all.20 = bf16[32,8,1024]{2,1,0:T(8,128)(2,1)S(1)} all-to-all(bf16[32,8,1024]{2,1,0:T(8,128)(2,1)S(1)} %bitcast.99), channel_id=1, replica_groups=mesh['ctx'=32,'head'=8] {'ctx'}, dimensions={0} | all-to-all | bytes 1048576 | tf_op jit(solution)/shard_map/all_to_all | solution.py:67
  85.2 1.8 stack.2
  87.0 5.4 %all-to-all-start.2 = ((bf16[32,256,128]{2,1,0:T(8,128)(2,1)}), bf16[32,256,128]{2,1,0:T(8,128)(2,1)S(1)}, u32[]{:S(2)}, u32[]{:S(2)}) async-start(bf16[32,256,128]{2,1,0:T(8,128)(2,1)} %stack.2), calls=%async_computation.2 | async-start | bytes 4194304 | tf_op jit(solution)/shard_map/all_to_all | solution.py:102
  97.2 23.8 %all-to-all-done.2 = bf16[32,256,128]{2,1,0:T(8,128)(2,1)S(1)} async-done(((bf16[32,256,128]{2,1,0:T(8,128)(2,1)}), bf16[32,256,128]{2,1,0:T(8,128)(2,1)S(1)}, u32[]{:S(2)}, u32[]{:S(2)}) %all-to-all-start.2) | async-done | bytes 2097184 | tf_op jit(solution)/shard_map/all_to_all | solution.py:102
  120.9 5.5 %all-gather.2.cloned.1.call-done = bf16[8192,128]{1,0:T(8,128)(2,1)} async-done(((bf16[256,128]{1,0:T(8,128)(2,1)}), bf16[8192,128]{1,0:T(8,128)(2,1)}) %all-gather.2.cloned.1.call-update) | async-done | bytes 2097168 | tf_op jit(solution)/shard_map/all_gather | solution.py:107
  126.4 81.7 %conditional.1 = (f32[1,8,256]{2,1,0:T(8,128)S(1)}, f32[1,8,256,128]{2,3,1,0:T(8,128)}) conditional(s32[]{:T(128)} %convert_element_type.43, () %tuple.13, (s32[256]{0:T(256)S(1)}, s32[256]{0:T(256)S(1)}, s32[32]{0:T(128)S(1)}, pred[256]{0:T(512)(128)(4,1)S(1)}, bf16[32,8,1024]{2,1,0:T(8,128)(2,1)S(1)}, /*index=5*/s32[256,1]{0,1:T(1,128)S(1)}, ...), branch_computations={%region_9.10_spmd, %region_10.14_spmd} | conditional | flops 8782093312 | bytes 227705264 | solution.py:119
  126.4 2.0 gather_fusion
  128.6 1.9 fusion.7
  130.5 26.9 %fusion.2 = (f32[8,256]{1,0:T(8,128)S(1)}, f32[256,8,8192]{2,0,1:T(8,128)}) fusion(pred[256,8192]{1,0:T(8,128)(4,1)S(1)} %fusion.7, bf16[8192,128,1]{1,0,2:T(8,128)(2,1)} %bitcast.100, bf16[256,1024]{1,0:T(8,128)(2,1)} %gather_fusion, bf16[256,1024]{1,0:T(8,128)(2,1)} %get-tuple-element.42, pred[256]{0:T(512)(128)(4,1)S(1)} %get-tuple-element.31), kind=kOutput, calls=%fused_computation.11 | convolution fusion | flops 4345559040 | bytes 72360192 | tf_op jit(solution)/shard_map/cond/branch_1_fun/qhgd,khd->hgqk/dot_general | solution.py:18
  157.4 26.3 %fusion.14 = f32[1,8,256,128]{3,2,1,0:T(8,128)} fusion(bf16[8192,128]{1,0:T(8,128)(2,1)} %get-tuple-element.36, f32[256,8,8192]{2,0,1:T(8,128)} %get-tuple-element.49, f32[8,256]{1,0:T(8,128)S(1)} %get-tuple-element.47, pred[256,8192]{1,0:T(8,128)(4,1)S(1)} %fusion.7, f32[8,256]{1,0:T(8,128)S(1)} %get-tuple-element.46), kind=kOutput, calls=%fused_computation.19 | convolution fusion | flops 4362338304 | bytes 72368128 | tf_op jit(solution)/shard_map/cond/branch_1_fun/hgqk,khd->hgqd/dot_general | solution.py:34
  183.7 21.8 %fusion.1 = f32[8,256]{1,0:T(8,128)S(1)} fusion(f32[256,8,8192]{2,0,1:T(8,128)} %get-tuple-element.49, f32[8,256]{1,0:T(8,128)S(1)} %get-tuple-element.47, pred[256,8192]{1,0:T(8,128)(4,1)S(1)} %fusion.7), kind=kLoop, calls=%fused_computation.10 | loop fusion | flops 67106816 | bytes 69222400 | tf_op jit(solution)/shard_map/cond/branch_1_fun/reduce_sum | solution.py:33
  205.5 2.6 copy.34
  208.0 1.3 divide_convert_fusion
  209.4 7.1 %convolution_convert_fusion = bf16[256,4096]{1,0:T(8,128)(2,1)} fusion(bf16[256,1024]{0,1:T(8,128)(2,1)S(1)} %bitcast.98, bf16[1024,4096]{1,0:T(8,128)(2,1)} %param.19), kind=kOutput, calls=%fused_computation.36 | convolution fusion | flops 2148532224 | bytes 11010048 | tf_op jit(solution)/shard_map/dot_general | solution.py:128
  216.5 44.1 %reduce-scatter.2.cloned.1.call-done = bf16[32,4096]{1,0:T(8,128)(2,1)} async-done(((bf16[256,4096]{1,0:T(8,128)(2,1)}), bf16[32,4096]{1,0:T(8,128)(2,1)}) %reduce-scatter.2.cloned.1.call-update) | async-done | bytes 262160 | tf_op jit(solution)/shard_map/reduce_scatter | solution.py:127
  (44 shorter events, 9.2 us)
Async XLA Ops:
  6.5 63.2 %copy-start = (bf16[256,1024]{1,0:T(8,128)(2,1)S(1)}, bf16[256,1024]{1,0:T(8,128)(2,1)}, u32[]{:S(2)}) copy-start(bf16[256,1024]{1,0:T(8,128)(2,1)} %param.14) | copy-start | bytes 1572868
  41.9 14.0 %all-to-all-start.3 = ((bf16[32,8,128]{2,1,0:T(8,128)(2,1)}), bf16[32,8,128]{2,1,0:T(8,128)(2,1)S(1)}, u32[]{:S(2)}, u32[]{:S(2)}) async-start(bf16[32,8,128]{2,1,0:T(8,128)(2,1)} %bitcast.23), calls=%async_computation.3 | async-start | bytes 131072 | tf_op jit(solution)/shard_map/all_to_all | solution.py:69
  55.8 11.4 %all-to-all-start.1 = ((bf16[32,8,128]{2,1,0:T(8,128)(2,1)}), bf16[32,8,128]{2,1,0:T(8,128)(2,1)S(1)}, u32[]{:S(2)}, u32[]{:S(2)}) async-start(bf16[32,8,128]{2,1,0:T(8,128)(2,1)} %bitcast.21), calls=%async_computation.1 | async-start | bytes 131072 | tf_op jit(solution)/shard_map/all_to_all | solution.py:68
  60.8 65.6 %all-gather.2.cloned.1.call-start = ((), (), s32[]{:S(2)}) async-start(), calls=%async_computation.5 | async-start | bytes 2162688 | tf_op jit(solution)/shard_map/all_gather | solution.py:107
  87.0 33.9 %all-to-all-start.2 = ((bf16[32,256,128]{2,1,0:T(8,128)(2,1)}), bf16[32,256,128]{2,1,0:T(8,128)(2,1)S(1)}, u32[]{:S(2)}, u32[]{:S(2)}) async-start(bf16[32,256,128]{2,1,0:T(8,128)(2,1)} %stack.2), calls=%async_computation.2 | async-start | bytes 4194304 | tf_op jit(solution)/shard_map/all_to_all | solution.py:102
  92.5 168.1 %reduce-scatter.2.cloned.1.call-start = ((), (), s32[]{:S(2)}) async-start(), calls=%async_computation.6 | async-start | bytes 2359296 | tf_op jit(solution)/shard_map/reduce_scatter | solution.py:127
  126.4 2.0 copy-start.1
Sparse Core Ops, SparseCore 0:
  69.8 56.5 all-gather.1
  216.6 43.9 reduce-scatter.1
